TPU v7x, 32 devices: a whole 2x2x4 slice. The times are simulated.
32 devices in a mesh: tm: 4 (over z), space: 8 (over y, x, core).
Axes of the slice: x: 2, y: 2, z: 4, core: 2. Of those that a mesh axis runs over, the one named last changes fastest.
Arguments:
- iterate: float32 [4, 8, 16, 16, 512], P('tm', 'space'), may hold values from -3 to 3
- source_term: float32 [4, 8, 16, 16, 512], P('tm', 'space'), may hold values from -6 to 6
- conductivity: float32 [8, 16, 16, 512], P('space'), may hold values from 0.5 to 4
Outputs:
- new_iterate: float32 [4, 8, 16, 16, 512], P('tm', 'space')
- residual: float32 [4, 8, 16, 16, 512], P('tm', 'space')
All inputs are finite; a program needn't handle non-finite values.
Results may differ from a plain program's by a relative error of at most 0.00002.
Values sent between devices are 32-bit elements; how exact they have to be, the bound alone decides.
A program may use at most 64 MiB of HBM per device.

v0:
```python
import jax
import jax.numpy as jnp
from jax import lax
from jax.sharding import PartitionSpec as P

tau_step = 0.08
damping = 0.7


def shifted(block, axis, distance):
    devices = range(lax.axis_size(axis))
    route = [(i - distance, i) for i in devices if i - distance in devices]
    return lax.ppermute(block, axis, route)


def from_partner(value, axis, stride):
    mask = 2**stride
    pairs = [(source, source ^ mask) for source in range(lax.axis_size(axis))]
    return lax.ppermute(value, axis, pairs)


def neighbours(grid_field):
    below_rows = shifted(grid_field[..., -1:, :], "space", 1)
    above_rows = shifted(grid_field[..., :1, :], "space", -1)
    zero_col = jnp.zeros_like(grid_field[..., :1])
    zero_plane = jnp.zeros_like(grid_field[..., :1, :, :])
    return [
        jnp.concatenate([below_rows, grid_field[..., :-1, :]], axis=-2),
        jnp.concatenate([grid_field[..., 1:, :], above_rows], axis=-2),
        jnp.concatenate([zero_col, grid_field[..., :-1]], axis=-1),
        jnp.concatenate([grid_field[..., 1:], zero_col], axis=-1),
        jnp.concatenate([zero_plane, grid_field[..., :-1, :, :]], axis=-3),
        jnp.concatenate([grid_field[..., 1:, :, :], zero_plane], axis=-3),
    ]


def weights_from(conduct, conduct_near):
    weights = [0.5 * (conduct + other) for other in conduct_near]
    weight_sum = weights[0]
    for near_item in weights[1:]:
        weight_sum = weight_sum + near_item
    return (weights, weight_sum)


def earlier(grid_field, depth_level):
    if depth_level == 0:
        return shifted(grid_field, "tm", 1)
    if depth_level == 1:
        return shifted(grid_field, "tm", 2)
    return shifted(grid_field, "tm", 4)


def operator_from(update, near_list, previous, weights, weight_sum, step_size):
    flux_sum = weights[0] * near_list[0]
    for position in range(1, 6):
        flux_sum = flux_sum + weights[position] * near_list[position]
    return update - previous + step_size * (weight_sum * update - flux_sum)


def apply_operator(update, weights, weight_sum, step_size, depth_level):
    return operator_from(
        update, neighbours(update), earlier(update, depth_level), weights, weight_sum, step_size
    )


def smooth(rhs_field, weights, weight_sum, step_size, depth_level, want_left):
    diag_term = 1.0 + step_size * weight_sum
    update = damping * rhs_field / diag_term
    update = (
        update
        + damping
        * (rhs_field - apply_operator(update, weights, weight_sum, step_size, depth_level))
        / diag_term
    )
    if want_left:
        return (
            update,
            rhs_field - apply_operator(update, weights, weight_sum, step_size, depth_level),
        )
    return (update, update)


def level_weights(conduct):
    return weights_from(conduct, neighbours(conduct))


def shards(iterate, source_term, conductivity):
    state_here = iterate[0, 0]
    source_here = source_term[0, 0]
    conduct = conductivity[0] * (1.0 + state_here * state_here)
    both_near = neighbours(jnp.stack([state_here, conduct]))
    state_near = [near_item[0] for near_item in both_near]
    conduct_near = [near_item[1] for near_item in both_near]
    weights, weight_sum = weights_from(conduct, conduct_near)
    residual = source_here - operator_from(
        state_here, state_near, earlier(state_here, 0), weights, weight_sum, tau_step
    )
    fine_update, fine_left = smooth(residual, weights, weight_sum, tau_step, 0, True)
    partner = from_partner((fine_left, conduct), "tm", 0)
    mid_rhs = partner[0] + fine_left
    mid_conduct = 0.5 * (partner[1] + conduct)
    mid_weights, mid_sum = level_weights(mid_conduct)
    mid_update, mid_left = smooth(mid_rhs, mid_weights, mid_sum, 2.0 * tau_step, 1, True)
    partner_mid = from_partner((mid_left, mid_conduct), "tm", 1)
    top_rhs = partner_mid[0] + mid_left
    top_conduct = 0.5 * (partner_mid[1] + mid_conduct)
    top_weights, top_sum = level_weights(top_conduct)
    top_update, unused = smooth(top_rhs, top_weights, top_sum, 4.0 * tau_step, 2, False)
    mid_update = mid_update + top_update
    fine_update = fine_update + mid_update
    new_state = state_here + fine_update
    return (new_state[None, None], residual[None, None])


def solution(mesh):
    in_specs = (
        P("tm", "space", None, None, None),
        P("tm", "space", None, None, None),
        P("space", None, None, None),
    )
    out_specs = (P("tm", "space", None, None, None), P("tm", "space", None, None, None))
    return jax.shard_map(shards, mesh=mesh, in_specs=in_specs, out_specs=out_specs, check_vma=False)
```

profile of v0, /device:TPU:25, one launch (start us, length us, event | category | flops | bytes accessed | tf_op | source)
XLA Modules:
  0.0 180.7 jit_solution(2721193868168687957)
XLA Ops:
  2.1 3.7 %collective-permute-start.1 = (f32[2,16,1,512]{3,2,1,0:T(1,128)S(1)}, f32[2,16,1,512]{3,2,1,0:T(1,128)S(1)}, u32[]{:S(2)}, u32[]{:S(2)}) collective-permute-start(f32[2,16,1,512]{3,2,1,0:T(1,128)S(1)} %get-tuple-element.17), channel_id=1, source_target_pairs={{0,1},{1,2},{2,3},{3,4},{4,5},{5,6},{6,7},{8,9},{9,10},{10,11},{11... | collective-permute-start | bytes 196616 | tf_op jit(solution)/shard_map/ppermute | solution.py:13
  11.7 10.2 %collective-permute-done = f32[16,16,512]{2,1,0:T(8,128)S(1)} collective-permute-done((f32[16,16,512]{2,1,0:T(8,128)S(1)}, f32[16,16,512]{2,1,0:T(8,128)S(1)}, u32[]{:S(2)}, u32[]{:S(2)}) %collective-permute-start) | collective-permute-done | bytes 524320 | tf_op jit(solution)/shard_map/ppermute | solution.py:13
  25.2 5.1 %collective-permute-start.4 = (f32[16,1,512]{2,1,0:T(1,128)S(1)}, f32[16,1,512]{2,1,0:T(1,128)S(1)}, u32[]{:S(2)}, u32[]{:S(2)}) collective-permute-start(f32[16,1,512]{2,1,0:T(1,128)S(1)} %get-tuple-element.80), channel_id=1, source_target_pairs={{0,1},{1,2},{2,3},{3,4},{4,5},{5,6},{6,7},{8,9},{9,10},{10,11},{11... | collective-permute-start | bytes 98312 | tf_op jit(solution)/shard_map/ppermute | solution.py:13
  32.5 2.4 %collective-permute-start.10 = (f32[16,16,512]{2,1,0:T(8,128)S(1)}, f32[16,16,512]{2,1,0:T(8,128)S(1)}, u32[]{:S(2)}, u32[]{:S(2)}) collective-permute-start(f32[16,16,512]{2,1,0:T(8,128)S(1)} %get-tuple-element.16), channel_id=1, source_target_pairs={{0,8},{8,0},{16,24},{24,16},{1,9},{9,1},{17,25},{25,17},{2,10},{10... | collective-permute-start | bytes 1572872 | tf_op jit(solution)/shard_map/ppermute | solution.py:19
  35.8 3.9 %collective-permute-done.3 = f32[16,16,512]{2,1,0:T(8,128)S(1)} collective-permute-done((f32[16,16,512]{2,1,0:T(8,128)S(1)}, f32[16,16,512]{2,1,0:T(8,128)S(1)}, u32[]{:S(2)}, u32[]{:S(2)}) %collective-permute-start.3) | collective-permute-done | bytes 524320 | tf_op jit(solution)/shard_map/ppermute | solution.py:13
  42.3 6.0 %collective-permute-start.7 = (f32[16,1,512]{2,1,0:T(1,128)S(1)}, f32[16,1,512]{2,1,0:T(1,128)S(1)}, u32[]{:S(2)}, u32[]{:S(2)}) collective-permute-start(f32[16,1,512]{2,1,0:T(1,128)S(1)} %get-tuple-element.64), channel_id=1, source_target_pairs={{0,1},{1,2},{2,3},{3,4},{4,5},{5,6},{6,7},{8,9},{9,10},{10,11},{11... | collective-permute-start | bytes 98312 | tf_op jit(solution)/shard_map/ppermute | solution.py:13
  51.3 6.0 %collective-permute-start.11 = (f32[16,1,512]{2,1,0:T(1,128)S(1)}, f32[16,1,512]{2,1,0:T(1,128)S(1)}, u32[]{:S(2)}, u32[]{:S(2)}) collective-permute-start(f32[16,1,512]{2,1,0:T(1,128)S(1)} %get-tuple-element.65), channel_id=1, source_target_pairs={{0,1},{1,2},{2,3},{3,4},{4,5},{5,6},{6,7},{8,9},{9,10},{10,11},{11... | collective-permute-start | bytes 98312 | tf_op jit(solution)/shard_map/ppermute | solution.py:13
  59.2 2.4 %collective-permute-done.6 = f32[16,16,512]{2,1,0:T(8,128)S(1)} collective-permute-done((f32[16,16,512]{2,1,0:T(8,128)S(1)}, f32[16,16,512]{2,1,0:T(8,128)S(1)}, u32[]{:S(2)}, u32[]{:S(2)}) %collective-permute-start.6) | collective-permute-done | bytes 524320 | tf_op jit(solution)/shard_map/ppermute | solution.py:13
  63.1 22.6 %collective-permute-done.9 = f32[16,16,512]{2,1,0:T(8,128)S(1)} collective-permute-done((f32[16,16,512]{2,1,0:T(8,128)S(1)}, f32[16,16,512]{2,1,0:T(8,128)S(1)}, u32[]{:S(2)}, u32[]{:S(2)}) %collective-permute-start.9) | collective-permute-done | bytes 524320 | tf_op jit(solution)/shard_map/ppermute | solution.py:19
  88.0 3.5 %collective-permute-start.14 = (f32[16,1,512]{2,1,0:T(1,128)S(1)}, f32[16,1,512]{2,1,0:T(1,128)S(1)}, u32[]{:S(2)}, u32[]{:S(2)}) collective-permute-start(f32[16,1,512]{2,1,0:T(1,128)S(1)} %get-tuple-element.56), channel_id=1, source_target_pairs={{0,1},{1,2},{2,3},{3,4},{4,5},{5,6},{6,7},{8,9},{9,10},{10,11},{11... | collective-permute-start | bytes 98312 | tf_op jit(solution)/shard_map/ppermute | solution.py:13
  93.6 3.1 %collective-permute-done.15 = f32[16,1,512]{2,1,0:T(1,128)S(1)} collective-permute-done((f32[16,1,512]{2,1,0:T(1,128)S(1)}, f32[16,1,512]{2,1,0:T(1,128)S(1)}, u32[]{:S(2)}, u32[]{:S(2)}) %collective-permute-start.15) | collective-permute-done | bytes 32800 | tf_op jit(solution)/shard_map/ppermute | solution.py:13
  96.7 39.2 %collective-permute-done.13 = f32[16,16,512]{2,1,0:T(8,128)S(1)} collective-permute-done((f32[16,16,512]{2,1,0:T(8,128)S(1)}, f32[16,16,512]{2,1,0:T(8,128)S(1)}, u32[]{:S(2)}, u32[]{:S(2)}) %collective-permute-start.13) | collective-permute-done | bytes 524320 | tf_op jit(solution)/shard_map/ppermute | solution.py:13
  138.7 2.3 %collective-permute-start.17 = (f32[16,1,512]{2,1,0:T(1,128)S(1)}, f32[16,1,512]{2,1,0:T(1,128)S(1)}, u32[]{:S(2)}, u32[]{:S(2)}) collective-permute-start(f32[16,1,512]{2,1,0:T(1,128)S(1)} %get-tuple-element.40), channel_id=1, source_target_pairs={{0,1},{1,2},{2,3},{3,4},{4,5},{5,6},{6,7},{8,9},{9,10},{10,11},{11... | collective-permute-start | bytes 98312 | tf_op jit(solution)/shard_map/ppermute | solution.py:13
  141.0 2.0 %collective-permute-start.18 = (f32[16,1,512]{2,1,0:T(1,128)S(1)}, f32[16,1,512]{2,1,0:T(1,128)S(1)}, u32[]{:S(2)}, u32[]{:S(2)}) collective-permute-start(f32[16,1,512]{2,1,0:T(1,128)S(1)} %get-tuple-element.39), channel_id=1, source_target_pairs={{1,0},{2,1},{3,2},{4,3},{5,4},{6,5},{7,6},{9,8},{10,9},{11,10},{12... | collective-permute-start | bytes 98312 | tf_op jit(solution)/shard_map/ppermute | solution.py:13
  143.3 3.3 %collective-permute-done.18 = f32[16,1,512]{2,1,0:T(1,128)S(1)} collective-permute-done((f32[16,1,512]{2,1,0:T(1,128)S(1)}, f32[16,1,512]{2,1,0:T(1,128)S(1)}, u32[]{:S(2)}, u32[]{:S(2)}) %collective-permute-start.18) | collective-permute-done | bytes 32800 | tf_op jit(solution)/shard_map/ppermute | solution.py:13
  146.6 6.6 %collective-permute-done.16 = f32[16,16,512]{2,1,0:T(8,128)S(1)} collective-permute-done((f32[16,16,512]{2,1,0:T(8,128)S(1)}, f32[16,16,512]{2,1,0:T(8,128)S(1)}, u32[]{:S(2)}, u32[]{:S(2)}) %collective-permute-start.16) | collective-permute-done | bytes 524320 | tf_op jit(solution)/shard_map/ppermute | solution.py:13
  154.7 3.2 %collective-permute-start.21 = (f32[16,1,512]{2,1,0:T(1,128)S(1)}, f32[16,1,512]{2,1,0:T(1,128)S(1)}, u32[]{:S(2)}, u32[]{:S(2)}) collective-permute-start(f32[16,1,512]{2,1,0:T(1,128)S(1)} %get-tuple-element.41), channel_id=1, source_target_pairs={{0,1},{1,2},{2,3},{3,4},{4,5},{5,6},{6,7},{8,9},{9,10},{10,11},{11... | collective-permute-start | bytes 98312 | tf_op jit(solution)/shard_map/ppermute | solution.py:13
  157.8 2.1 %collective-permute-start.22 = (f32[16,1,512]{2,1,0:T(1,128)S(1)}, f32[16,1,512]{2,1,0:T(1,128)S(1)}, u32[]{:S(2)}, u32[]{:S(2)}) collective-permute-start(f32[16,1,512]{2,1,0:T(1,128)S(1)} %get-tuple-element.42), channel_id=1, source_target_pairs={{1,0},{2,1},{3,2},{4,3},{5,4},{6,5},{7,6},{9,8},{10,9},{11,10},{12... | collective-permute-start | bytes 98312 | tf_op jit(solution)/shard_map/ppermute | solution.py:13
  160.3 3.1 %collective-permute-done.22 = f32[16,1,512]{2,1,0:T(1,128)S(1)} collective-permute-done((f32[16,1,512]{2,1,0:T(1,128)S(1)}, f32[16,1,512]{2,1,0:T(1,128)S(1)}, u32[]{:S(2)}, u32[]{:S(2)}) %collective-permute-start.22) | collective-permute-done | bytes 32800 | tf_op jit(solution)/shard_map/ppermute | solution.py:13
  163.4 4.3 %collective-permute-done.19 = f32[16,16,512]{2,1,0:T(8,128)S(1)} collective-permute-done((f32[16,16,512]{2,1,0:T(8,128)S(1)}, f32[16,16,512]{2,1,0:T(8,128)S(1)}, u32[]{:S(2)}, u32[]{:S(2)}) %collective-permute-start.19) | collective-permute-done | bytes 524320 | tf_op jit(solution)/shard_map/ppermute | solution.py:19
  169.2 4.0 %collective-permute-start.24 = (f32[16,1,512]{2,1,0:T(1,128)S(1)}, f32[16,1,512]{2,1,0:T(1,128)S(1)}, u32[]{:S(2)}, u32[]{:S(2)}) collective-permute-start(f32[16,1,512]{2,1,0:T(1,128)S(1)} %get-tuple-element.23), channel_id=1, source_target_pairs={{0,1},{1,2},{2,3},{3,4},{4,5},{5,6},{6,7},{8,9},{9,10},{10,11},{11... | collective-permute-start | bytes 98312 | tf_op jit(solution)/shard_map/ppermute | solution.py:13
  173.2 1.9 %collective-permute-start.25 = (f32[16,1,512]{2,1,0:T(1,128)S(1)}, f32[16,1,512]{2,1,0:T(1,128)S(1)}, u32[]{:S(2)}, u32[]{:S(2)}) collective-permute-start(f32[16,1,512]{2,1,0:T(1,128)S(1)} %get-tuple-element.24), channel_id=1, source_target_pairs={{1,0},{2,1},{3,2},{4,3},{5,4},{6,5},{7,6},{9,8},{10,9},{11,10},{12... | collective-permute-start | bytes 98312 | tf_op jit(solution)/shard_map/ppermute | solution.py:13
  175.5 3.0 %collective-permute-done.25 = f32[16,1,512]{2,1,0:T(1,128)S(1)} collective-permute-done((f32[16,1,512]{2,1,0:T(1,128)S(1)}, f32[16,1,512]{2,1,0:T(1,128)S(1)}, u32[]{:S(2)}, u32[]{:S(2)}) %collective-permute-start.25) | collective-permute-done | bytes 32800 | tf_op jit(solution)/shard_map/ppermute | solution.py:13
  178.5 2.2 %fusion.108 = f32[1,1,16,16,512]{4,3,2,1,0:T(8,128)} fusion(f32[16,16,512]{2,1,0:T(8,128)S(1)} %fusion.55, f32[16,16,512]{2,1,0:T(8,128)S(1)} %fusion.78, f32[16,16,512]{2,1,0:T(8,128)S(1)} %get-tuple-element.3, f32[15,16,512]{2,1,0:T(8,128)S(1)} %get-tuple-element.30, f32[15,16,512]{2,1,0:T(8,128)S(1)} %get-tuple-element.29, ...), kind=kLoop, calls=%fused_computation.168 | loop fusion | flops 6291456 | bytes 9826304 | tf_op jit(solution)/shard_map/broadcast_in_dim | solution.py:112
  (79 shorter events, 33.6 us)
Async XLA Ops:
  2.1 7.7 %collective-permute-start.1 = (f32[2,16,1,512]{3,2,1,0:T(1,128)S(1)}, f32[2,16,1,512]{3,2,1,0:T(1,128)S(1)}, u32[]{:S(2)}, u32[]{:S(2)}) collective-permute-start(f32[2,16,1,512]{3,2,1,0:T(1,128)S(1)} %get-tuple-element.17), channel_id=1, source_target_pairs={{0,1},{1,2},{2,3},{3,4},{4,5},{5,6},{6,7},{8,9},{9,10},{10,11},{11... | collective-permute-start | bytes 196616 | tf_op jit(solution)/shard_map/ppermute | solution.py:13
  5.8 5.9 %collective-permute-start.2 = (f32[2,16,1,512]{3,2,1,0:T(1,128)S(1)}, f32[2,16,1,512]{3,2,1,0:T(1,128)S(1)}, u32[]{:S(2)}, u32[]{:S(2)}) collective-permute-start(f32[2,16,1,512]{3,2,1,0:T(1,128)S(1)} %get-tuple-element.18), channel_id=1, source_target_pairs={{1,0},{2,1},{3,2},{4,3},{5,4},{6,5},{7,6},{9,8},{10,9},{11,10},{12... | collective-permute-start | bytes 196616 | tf_op jit(solution)/shard_map/ppermute | solution.py:13
  7.7 14.1 %collective-permute-start = (f32[16,16,512]{2,1,0:T(8,128)S(1)}, f32[16,16,512]{2,1,0:T(8,128)S(1)}, u32[]{:S(2)}, u32[]{:S(2)}) collective-permute-start(f32[16,16,512]{2,1,0:T(8,128)S(1)} %bitcast.118), channel_id=1, source_target_pairs={{0,8},{8,16},{16,24},{1,9},{9,17},{17,25},{2,10},{10,18},{18,26},{... | collective-permute-start | bytes 1572872 | tf_op jit(solution)/shard_map/ppermute | solution.py:13
  23.9 15.8 %collective-permute-start.3 = (f32[16,16,512]{2,1,0:T(8,128)S(1)}, f32[16,16,512]{2,1,0:T(8,128)S(1)}, u32[]{:S(2)}, u32[]{:S(2)}) collective-permute-start(f32[16,16,512]{2,1,0:T(8,128)S(1)} %get-tuple-element.8), channel_id=1, source_target_pairs={{0,8},{8,16},{16,24},{1,9},{9,17},{17,25},{2,10},{10,18},{18,26},{... | collective-permute-start | bytes 1572872 | tf_op jit(solution)/shard_map/ppermute | solution.py:13
  25.2 9.7 %collective-permute-start.4 = (f32[16,1,512]{2,1,0:T(1,128)S(1)}, f32[16,1,512]{2,1,0:T(1,128)S(1)}, u32[]{:S(2)}, u32[]{:S(2)}) collective-permute-start(f32[16,1,512]{2,1,0:T(1,128)S(1)} %get-tuple-element.80), channel_id=1, source_target_pairs={{0,1},{1,2},{2,3},{3,4},{4,5},{5,6},{6,7},{8,9},{9,10},{10,11},{11... | collective-permute-start | bytes 98312 | tf_op jit(solution)/shard_map/ppermute | solution.py:13
  30.3 5.5 %collective-permute-start.5 = (f32[16,1,512]{2,1,0:T(1,128)S(1)}, f32[16,1,512]{2,1,0:T(1,128)S(1)}, u32[]{:S(2)}, u32[]{:S(2)}) collective-permute-start(f32[16,1,512]{2,1,0:T(1,128)S(1)} %get-tuple-element.79), channel_id=1, source_target_pairs={{1,0},{2,1},{3,2},{4,3},{5,4},{6,5},{7,6},{9,8},{10,9},{11,10},{12... | collective-permute-start | bytes 98312 | tf_op jit(solution)/shard_map/ppermute | solution.py:13
  32.5 18.5 %collective-permute-start.10 = (f32[16,16,512]{2,1,0:T(8,128)S(1)}, f32[16,16,512]{2,1,0:T(8,128)S(1)}, u32[]{:S(2)}, u32[]{:S(2)}) collective-permute-start(f32[16,16,512]{2,1,0:T(8,128)S(1)} %get-tuple-element.16), channel_id=1, source_target_pairs={{0,8},{8,0},{16,24},{24,16},{1,9},{9,1},{17,25},{25,17},{2,10},{10... | collective-permute-start | bytes 1572872 | tf_op jit(solution)/shard_map/ppermute | solution.py:19
  40.9 20.7 %collective-permute-start.6 = (f32[16,16,512]{2,1,0:T(8,128)S(1)}, f32[16,16,512]{2,1,0:T(8,128)S(1)}, u32[]{:S(2)}, u32[]{:S(2)}) collective-permute-start(f32[16,16,512]{2,1,0:T(8,128)S(1)} %fusion.55), channel_id=1, source_target_pairs={{0,8},{8,16},{16,24},{1,9},{9,17},{17,25},{2,10},{10,18},{18,26},{... | collective-permute-start | bytes 1572872 | tf_op jit(solution)/shard_map/ppermute | solution.py:13
  42.3 17.0 %collective-permute-start.7 = (f32[16,1,512]{2,1,0:T(1,128)S(1)}, f32[16,1,512]{2,1,0:T(1,128)S(1)}, u32[]{:S(2)}, u32[]{:S(2)}) collective-permute-start(f32[16,1,512]{2,1,0:T(1,128)S(1)} %get-tuple-element.64), channel_id=1, source_target_pairs={{0,1},{1,2},{2,3},{3,4},{4,5},{5,6},{6,7},{8,9},{9,10},{10,11},{11... | collective-permute-start | bytes 98312 | tf_op jit(solution)/shard_map/ppermute | solution.py:13
  48.2 11.0 %collective-permute-start.8 = (f32[16,1,512]{2,1,0:T(1,128)S(1)}, f32[16,1,512]{2,1,0:T(1,128)S(1)}, u32[]{:S(2)}, u32[]{:S(2)}) collective-permute-start(f32[16,1,512]{2,1,0:T(1,128)S(1)} %get-tuple-element.63), channel_id=1, source_target_pairs={{1,0},{2,1},{3,2},{4,3},{5,4},{6,5},{7,6},{9,8},{10,9},{11,10},{12... | collective-permute-start | bytes 98312 | tf_op jit(solution)/shard_map/ppermute | solution.py:13
  51.3 11.8 %collective-permute-start.11 = (f32[16,1,512]{2,1,0:T(1,128)S(1)}, f32[16,1,512]{2,1,0:T(1,128)S(1)}, u32[]{:S(2)}, u32[]{:S(2)}) collective-permute-start(f32[16,1,512]{2,1,0:T(1,128)S(1)} %get-tuple-element.65), channel_id=1, source_target_pairs={{0,1},{1,2},{2,3},{3,4},{4,5},{5,6},{6,7},{8,9},{9,10},{10,11},{11... | collective-permute-start | bytes 98312 | tf_op jit(solution)/shard_map/ppermute | solution.py:13
  57.3 5.8 %collective-permute-start.12 = (f32[16,1,512]{2,1,0:T(1,128)S(1)}, f32[16,1,512]{2,1,0:T(1,128)S(1)}, u32[]{:S(2)}, u32[]{:S(2)}) collective-permute-start(f32[16,1,512]{2,1,0:T(1,128)S(1)} %get-tuple-element.66), channel_id=1, source_target_pairs={{1,0},{2,1},{3,2},{4,3},{5,4},{6,5},{7,6},{9,8},{10,9},{11,10},{12... | collective-permute-start | bytes 98312 | tf_op jit(solution)/shard_map/ppermute | solution.py:13
  62.7 23.0 %collective-permute-start.9 = (f32[16,16,512]{2,1,0:T(8,128)S(1)}, f32[16,16,512]{2,1,0:T(8,128)S(1)}, u32[]{:S(2)}, u32[]{:S(2)}) collective-permute-start(f32[16,16,512]{2,1,0:T(8,128)S(1)} %fusion.64), channel_id=1, source_target_pairs={{0,8},{8,0},{16,24},{24,16},{1,9},{9,1},{17,25},{25,17},{2,10},{10... | collective-permute-start | bytes 1572872 | tf_op jit(solution)/shard_map/ppermute | solution.py:19
  62.9 80.4 %collective-permute-start.20 = (f32[16,16,512]{2,1,0:T(8,128)S(1)}, f32[16,16,512]{2,1,0:T(8,128)S(1)}, u32[]{:S(2)}, u32[]{:S(2)}) collective-permute-start(f32[16,16,512]{2,1,0:T(8,128)S(1)} %add_multiply_fusion.9), channel_id=1, source_target_pairs={{0,16},{8,24},{16,0},{24,8},{1,17},{9,25},{17,1},{25,9},{2,18},{10... | collective-permute-start | bytes 1572872 | tf_op jit(solution)/shard_map/ppermute | solution.py:19
  86.6 49.3 %collective-permute-start.13 = (f32[16,16,512]{2,1,0:T(8,128)S(1)}, f32[16,16,512]{2,1,0:T(8,128)S(1)}, u32[]{:S(2)}, u32[]{:S(2)}) collective-permute-start(f32[16,16,512]{2,1,0:T(8,128)S(1)} %get-tuple-element.4), channel_id=1, source_target_pairs={{0,16},{8,24},{1,17},{9,25},{2,18},{10,26},{3,19},{11,27},{4,20},{... | collective-permute-start | bytes 1572872 | tf_op jit(solution)/shard_map/ppermute | solution.py:13
  88.0 5.7 %collective-permute-start.14 = (f32[16,1,512]{2,1,0:T(1,128)S(1)}, f32[16,1,512]{2,1,0:T(1,128)S(1)}, u32[]{:S(2)}, u32[]{:S(2)}) collective-permute-start(f32[16,1,512]{2,1,0:T(1,128)S(1)} %get-tuple-element.56), channel_id=1, source_target_pairs={{0,1},{1,2},{2,3},{3,4},{4,5},{5,6},{6,7},{8,9},{9,10},{10,11},{11... | collective-permute-start | bytes 98312 | tf_op jit(solution)/shard_map/ppermute | solution.py:13
  137.4 15.8 %collective-permute-start.16 = (f32[16,16,512]{2,1,0:T(8,128)S(1)}, f32[16,16,512]{2,1,0:T(8,128)S(1)}, u32[]{:S(2)}, u32[]{:S(2)}) collective-permute-start(f32[16,16,512]{2,1,0:T(8,128)S(1)} %fusion.78), channel_id=1, source_target_pairs={{0,16},{8,24},{1,17},{9,25},{2,18},{10,26},{3,19},{11,27},{4,20},{... | collective-permute-start | bytes 1572872 | tf_op jit(solution)/shard_map/ppermute | solution.py:13
  141.0 5.5 %collective-permute-start.18 = (f32[16,1,512]{2,1,0:T(1,128)S(1)}, f32[16,1,512]{2,1,0:T(1,128)S(1)}, u32[]{:S(2)}, u32[]{:S(2)}) collective-permute-start(f32[16,1,512]{2,1,0:T(1,128)S(1)} %get-tuple-element.39), channel_id=1, source_target_pairs={{1,0},{2,1},{3,2},{4,3},{5,4},{6,5},{7,6},{9,8},{10,9},{11,10},{12... | collective-permute-start | bytes 98312 | tf_op jit(solution)/shard_map/ppermute | solution.py:13
  154.6 13.1 %collective-permute-start.19 = (f32[16,16,512]{2,1,0:T(8,128)S(1)}, f32[16,16,512]{2,1,0:T(8,128)S(1)}, u32[]{:S(2)}, u32[]{:S(2)}) collective-permute-start(f32[16,16,512]{2,1,0:T(8,128)S(1)} %get-tuple-element.31), channel_id=1, source_target_pairs={{0,16},{8,24},{16,0},{24,8},{1,17},{9,25},{17,1},{25,9},{2,18},{10... | collective-permute-start | bytes 1572872 | tf_op jit(solution)/shard_map/ppermute | solution.py:19
  154.7 5.6 %collective-permute-start.21 = (f32[16,1,512]{2,1,0:T(1,128)S(1)}, f32[16,1,512]{2,1,0:T(1,128)S(1)}, u32[]{:S(2)}, u32[]{:S(2)}) collective-permute-start(f32[16,1,512]{2,1,0:T(1,128)S(1)} %get-tuple-element.41), channel_id=1, source_target_pairs={{0,1},{1,2},{2,3},{3,4},{4,5},{5,6},{6,7},{8,9},{9,10},{10,11},{11... | collective-permute-start | bytes 98312 | tf_op jit(solution)/shard_map/ppermute | solution.py:13
  157.8 5.5 %collective-permute-start.22 = (f32[16,1,512]{2,1,0:T(1,128)S(1)}, f32[16,1,512]{2,1,0:T(1,128)S(1)}, u32[]{:S(2)}, u32[]{:S(2)}) collective-permute-start(f32[16,1,512]{2,1,0:T(1,128)S(1)} %get-tuple-element.42), channel_id=1, source_target_pairs={{1,0},{2,1},{3,2},{4,3},{5,4},{6,5},{7,6},{9,8},{10,9},{11,10},{12... | collective-permute-start | bytes 98312 | tf_op jit(solution)/shard_map/ppermute | solution.py:13
  168.5 10.0 %collective-permute-start.23 = (f32[16,16,512]{2,1,0:T(8,128)S(1)}, f32[16,16,512]{2,1,0:T(8,128)S(1)}, u32[]{:S(2)}, u32[]{:S(2)}) collective-permute-start(f32[16,16,512]{2,1,0:T(8,128)S(1)} %get-tuple-element.2), channel_id=1, source_target_pairs={} | collective-permute-start | bytes 1572872 | tf_op jit(solution)/shard_map/ppermute | solution.py:13
  169.2 6.3 %collective-permute-start.24 = (f32[16,1,512]{2,1,0:T(1,128)S(1)}, f32[16,1,512]{2,1,0:T(1,128)S(1)}, u32[]{:S(2)}, u32[]{:S(2)}) collective-permute-start(f32[16,1,512]{2,1,0:T(1,128)S(1)} %get-tuple-element.23), channel_id=1, source_target_pairs={{0,1},{1,2},{2,3},{3,4},{4,5},{5,6},{6,7},{8,9},{9,10},{10,11},{11... | collective-permute-start | bytes 98312 | tf_op jit(solution)/shard_map/ppermute | solution.py:13
  173.2 5.2 %collective-permute-start.25 = (f32[16,1,512]{2,1,0:T(1,128)S(1)}, f32[16,1,512]{2,1,0:T(1,128)S(1)}, u32[]{:S(2)}, u32[]{:S(2)}) collective-permute-start(f32[16,1,512]{2,1,0:T(1,128)S(1)} %get-tuple-element.24), channel_id=1, source_target_pairs={{1,0},{2,1},{3,2},{4,3},{5,4},{6,5},{7,6},{9,8},{10,9},{11,10},{12... | collective-permute-start | bytes 98312 | tf_op jit(solution)/shard_map/ppermute | solution.py:13
  (6 other events, 73.4 us)
where the time goes:
time: 181 us
  waiting for transfers between devices  105 us (58%)
  starting transfers between devices  59.2 us (33%)
  other arithmetic  12.2 us (7%)
  local copies, waits for them, and re-layouts  3.3 us (2%)
    ppermute x22, waiting for transfers between devices, shifted(): return lax.ppermute(block, axis, route)  77.4 us
    ppermute x22, starting transfers between devices, shifted(): return lax.ppermute(block, axis, route)  56.5 us
    ppermute x4, waiting for transfers between devices, from_partner(): return lax.ppermute(value, axis, pairs)  27.5 us
  transfers between devices with their start and end apart: 26, of which 14 were waited for; matrix products, arithmetic and copies ran while one was open for 4% of the time, Pallas kernels for 0%

commit v1 on v0

v1 whole, which is shorter than its diff:
```python
import functools

import jax
import jax.numpy as jnp
from jax import lax
from jax.experimental import pallas as pl
from jax.experimental.pallas import tpu as pltpu
from jax.sharding import PartitionSpec as P

tau_step = 0.08
damping = 0.7
group = 4
pad = 8
mesh_ids = pl.DeviceIdType.MESH

slots_state = [0, 2, 4, 6]
slots_one = [8, 9, 10, 11]
slots_two = [12, 13, 14, 15]
slots_mid_one = [16, 17]
slots_mid_two = [18, 19]
slot_top = 20
n_slots = 21


def kernel(
    tm_size, space_size,
    state_in, source_in, kappa_in, new_out, res_out,
    u, c, e1, e2, kap, src, res, wl, wr, rd,
    mc, me1, me2, mb, mwl, mwr, mrd, tc, te, tb, new,
    row_send, row_recv, col_send, col_recv,
    in_ssem, in_rsem, out_ssem, out_rsem, loc_sem, h_ssem, h_rsem, t_ssem, t_rsem,
):
    nz, tx, width = kap.shape
    real = pl.ds(pad, tx)
    low = pl.ds(pad - 1, tx)
    high = pl.ds(pad + 1, tx)
    planes = pl.ds(1, nz)
    me = lax.axis_index("tm")
    sp = lax.axis_index("space")
    q = me % group
    base = me - q
    chained = tm_size > group
    has_dn, has_up = sp > 0, sp < space_size - 1
    has_left, has_right = q > 0, q < group - 1
    has_prev, has_next = base > 0, base + group < tm_size
    sides = [
        (has_dn, {"space": sp - 1}),
        (has_up, {"space": sp + 1}),
        (has_left, {"tm": me - 1}),
        (has_right, {"tm": me + 1}),
    ]

    def zero_edges(ref, count):
        for n in range(count):
            for plane in (0, nz + 1):
                ref[n, plane] = jnp.zeros(ref.shape[2:], jnp.float32)

    zero_edges(u, group + 1)
    zero_edges(c, group)
    zero_edges(e1, group + 1)
    zero_edges(e2, group + 1)
    zero_edges(mc, 2)
    zero_edges(me1, 3)
    zero_edges(me2, 3)
    zero_edges(tc, 1)
    zero_edges(te, 2)

    @pl.when(jnp.logical_not(has_prev))
    def _():
        for ref in (u, e1, e2, me1, me2, te):
            ref[0] = jnp.zeros(ref.shape[1:], jnp.float32)

    for number, (has, _) in enumerate(sides):
        buffer = row_recv if number < 2 else col_recv

        @pl.when(jnp.logical_not(has))
        def _():
            buffer[number % 2] = jnp.zeros(buffer.shape[1:], jnp.float32)

    barrier = pltpu.get_barrier_semaphore()
    for j in range(1, group):
        pl.semaphore_signal(
            barrier, inc=1, device_id={"tm": base + (q + j) % group}, device_id_type=mesh_ids
        )
    greeted = [(has_dn, sides[0][1]), (has_up, sides[1][1])]
    if chained:
        greeted += [(has_prev, {"tm": me - group}), (has_next, {"tm": me + group})]
    for has, where in greeted:

        @pl.when(has)
        def _():
            pl.semaphore_signal(barrier, inc=1, device_id=where, device_id_type=mesh_ids)

    expected = group - 1
    for has, _ in greeted:
        expected = expected + jnp.where(has, 1, 0)
    pl.semaphore_wait(barrier, expected)

    def columns(d):
        return pl.ds(pl.multiple_of(d * width, width), width)

    def in_copy(a, j):
        d = (q + j) % group
        hbm = (state_in, source_in)[a].at[0, 0, :, :, columns(d)]
        dst = u.at[q + 1, planes, real, :] if a == 0 else src.at[q]
        if j == 0:
            return pltpu.make_async_copy(hbm, dst, loc_sem.at[a])
        return pltpu.make_async_remote_copy(
            src_ref=hbm, dst_ref=dst, send_sem=in_ssem.at[a, j - 1],
            recv_sem=in_rsem.at[a, j - 1], device_id={"tm": base + d}, device_id_type=mesh_ids,
        )

    def out_copy(a, j):
        d = (q + j) % group
        hbm = (res_out, new_out)[a].at[0, 0, :, :, columns(q)]
        own = (res, new)[a].at[d]
        if j == 0:
            return pltpu.make_async_copy(own, hbm, loc_sem.at[3 + a])
        return pltpu.make_async_remote_copy(
            src_ref=own, dst_ref=hbm, send_sem=out_ssem.at[a, j - 1],
            recv_sem=out_rsem.at[a, j - 1], device_id={"tm": base + d}, device_id_type=mesh_ids,
        )

    kappa_copy = pltpu.make_async_copy(
        kappa_in.at[0, :, :, columns(q)], kap, loc_sem.at[2]
    )
    kappa_copy.start()
    order = (2, 1, 3, 0)
    for a in range(2):
        for j in order:
            in_copy(a, j).start()

    def halo_copy(slot, count, number):
        part = pl.ds(slot, count)
        opposite = number ^ 1
        if number < 2:
            source, target = row_send.at[number, part], row_recv.at[opposite, part]
        else:
            source, target = col_send.at[part], col_recv.at[opposite - 2, part]
        return pltpu.make_async_remote_copy(
            src_ref=source, dst_ref=target, send_sem=h_ssem.at[number, slot],
            recv_sem=h_rsem.at[opposite, slot], device_id=sides[number][1],
            device_id_type=mesh_ids,
        )

    def halo_send(slot, count=1):
        for number in (2, 3, 0, 1):

            @pl.when(sides[number][0])
            def _():
                halo_copy(slot, count, number).start()

    def halo_wait(slot, count=1):
        part = pl.ds(slot, count)
        for number in range(4):
            target = row_recv.at[number, part] if number < 2 else col_recv.at[number - 2, part]

            @pl.when(sides[number][0])
            def _():
                pltpu.make_async_remote_copy(
                    src_ref=target, dst_ref=target, send_sem=h_ssem.at[number, slot],
                    recv_sem=h_rsem.at[number, slot], device_id=sides[number][1],
                    device_id_type=mesh_ids,
                ).wait_recv()

    def time_copy(number, ref, last):
        return pltpu.make_async_remote_copy(
            src_ref=ref.at[last, planes, real, :], dst_ref=ref.at[0, planes, real, :],
            send_sem=t_ssem.at[number],
            recv_sem=t_rsem.at[number], device_id={"tm": me + group}, device_id_type=mesh_ids,
        )

    time_refs = [(u, group), (e1, group), (e2, group), (me1, 2), (me2, 2), (te, 1)]

    def time_send(number):
        if chained:

            @pl.when(has_next)
            def _():
                time_copy(number, *time_refs[number]).start()

    def time_wait(number):
        if chained:

            @pl.when(has_prev)
            def _():
                time_copy(number, *time_refs[number]).wait_recv()

    lane = lax.broadcasted_iota(jnp.int32, (tx, width), 1)
    first_lane = lane == 0
    last_lane = lane == width - 1
    odd_lane = lane % 2 == 1
    pair_lane = lane // 2

    def pack(slot, p, value, packed):
        row_send[0, slot, pl.ds(p, 1), :] = value[:1]
        row_send[1, slot, pl.ds(p, 1), :] = value[tx - 1 :]
        return jnp.where(pair_lane == p, pltpu.roll(value, 2 * p + 1, 1), packed)

    def ghosts(slot):
        return jnp.where(
            odd_lane,
            pltpu.roll(col_recv[0, slot], 1, 1),
            pltpu.roll(col_recv[1, slot], width - 1, 1),
        )

    def put_rows(ref, n, slot, p):
        ref[n, p + 1, pl.ds(pad - 1, 1), :] = row_recv[0, slot, pl.ds(p, 1), :]
        ref[n, p + 1, pl.ds(pad + tx, 1), :] = row_recv[1, slot, pl.ds(p, 1), :]

    def sideways(value, ghost, p):
        edge = pltpu.roll(ghost, width - 1 - 2 * p, 1)
        left = jnp.where(first_lane, edge, pltpu.roll(value, 1, 1))
        right = jnp.where(last_lane, edge, pltpu.roll(value, width - 1, 1))
        return left, right

    def straight(ref, n, p):
        return (
            ref[n, p + 1, low, :], ref[n, p + 1, high, :],
            ref[n, p, real, :], ref[n, p + 2, real, :],
        )

    def flux(v, v_near, cc, c_near, left_w, right_w):
        total = left_w * (v - v_near[4]) + right_w * (v - v_near[5])
        for i in range(4):
            total = total + (cc + c_near[i]) * (v - v_near[i])
        return total

    def near_of(ref, n, slot, ghost, p):
        put_rows(ref, n, slot, p)
        v = ref[n, p + 1, real, :]
        return v, straight(ref, n, p) + sideways(v, ghost, p)

    def plane_loop(body, init):
        return lax.fori_loop(0, nz, body, init, unroll=2)

    blank = jnp.zeros((tx, width), jnp.float32)

    kappa_copy.wait()
    in_copy(0, 0).wait()
    for j in order[:3]:
        in_copy(0, j).wait_recv()
    time_send(0)
    for n in range(group):

        def body(p, packed):
            v = u[n + 1, p + 1, real, :]
            cc = kap[p] * (1.0 + v * v)
            c[n, p + 1, real, :] = cc
            slot = slots_state[n]
            return pack(slot, p, v, packed[0]), pack(slot + 1, p, cc, packed[1])

        packed = plane_loop(body, (blank, blank))
        col_send[slots_state[n]] = packed[0]
        col_send[slots_state[n] + 1] = packed[1]
        halo_send(slots_state[n], 2)

    half = 0.5 * tau_step
    for n in range(group):
        halo_wait(slots_state[n], 2)
        ghost_c = ghosts(slots_state[n] + 1)

        def body(p, carry):
            cc, c_near = near_of(c, n, slots_state[n] + 1, ghost_c, p)
            wl[n, p] = cc + c_near[4]
            wr[n, p] = cc + c_near[5]
            total = 6.0 * cc
            for item in c_near:
                total = total + item
            rd[n, p] = damping / (1.0 + half * total)
            return carry

        plane_loop(body, 0)

    in_copy(1, 0).wait()
    for j in order[:3]:
        in_copy(1, j).wait_recv()
    time_wait(0)
    for n in range(group):
        ghost_u = ghosts(slots_state[n])

        def body(p, packed):
            v, v_near = near_of(u, n + 1, slots_state[n], ghost_u, p)
            total = flux(v, v_near, c[n, p + 1, real, :], straight(c, n, p), wl[n, p], wr[n, p])
            left = src[n, p] - (v - u[n, p + 1, real, :] + half * total)
            res[n, p] = left
            update = left * rd[n, p]
            e1[n + 1, p + 1, real, :] = update
            return pack(slots_one[n], p, update, packed)

        col_send[slots_one[n]] = plane_loop(body, blank)
        halo_send(slots_one[n])
    time_send(1)

    for j in order:
        out_copy(0, j).start()

    time_wait(1)
    for n in range(group):
        halo_wait(slots_one[n])
        ghost = ghosts(slots_one[n])

        def body(p, packed):
            v, v_near = near_of(e1, n + 1, slots_one[n], ghost, p)
            total = flux(v, v_near, c[n, p + 1, real, :], straight(c, n, p), wl[n, p], wr[n, p])
            left = res[n, p] - (v - e1[n, p + 1, real, :] + half * total)
            update = v + left * rd[n, p]
            e2[n + 1, p + 1, real, :] = update
            return pack(slots_two[n], p, update, packed)

        col_send[slots_two[n]] = plane_loop(body, blank)
        halo_send(slots_two[n])
    time_send(2)

    def body(p, carry):
        for j in range(2):
            mc[j, p + 1] = 0.5 * (c[2 * j, p + 1] + c[2 * j + 1, p + 1])
            mwl[j, p] = 0.5 * (wl[2 * j, p] + wl[2 * j + 1, p])
            mwr[j, p] = 0.5 * (wr[2 * j, p] + wr[2 * j + 1, p])
        tc[0, p + 1] = 0.5 * (mc[0, p + 1] + mc[1, p + 1])
        return carry

    lax.fori_loop(0, nz, body, 0)

    def diagonal(ref, j, p, left_w, right_w, scale):
        cc = ref[j, p + 1, real, :]
        total = 4.0 * cc + left_w + right_w
        for item in straight(ref, j, p):
            total = total + item
        return damping / (1.0 + scale * total)

    time_wait(2)
    for j in range(2):
        halo_wait(slots_two[2 * j])
        halo_wait(slots_two[2 * j + 1])
        pair = [ghosts(slots_two[2 * j]), ghosts(slots_two[2 * j + 1])]

        def body(p, packed):
            rhs = None
            for i in range(2):
                n = 2 * j + i
                v, v_near = near_of(e2, n + 1, slots_two[n], pair[i], p)
                total = flux(
                    v, v_near, c[n, p + 1, real, :], straight(c, n, p), wl[n, p], wr[n, p]
                )
                left = res[n, p] - (v - e2[n, p + 1, real, :] + half * total)
                rhs = left if rhs is None else rhs + left
            inverse = diagonal(mc, j, p, mwl[j, p], mwr[j, p], 2.0 * half)
            mrd[j, p] = inverse
            mb[j, p] = rhs
            update = rhs * inverse
            me1[j + 1, p + 1, real, :] = update
            return pack(slots_mid_one[j], p, update, packed)

        col_send[slots_mid_one[j]] = plane_loop(body, blank)
        halo_send(slots_mid_one[j])
    time_send(3)

    time_wait(3)
    for j in range(2):
        halo_wait(slots_mid_one[j])
        ghost = ghosts(slots_mid_one[j])

        def body(p, packed):
            v, v_near = near_of(me1, j + 1, slots_mid_one[j], ghost, p)
            total = flux(v, v_near, mc[j, p + 1, real, :], straight(mc, j, p), mwl[j, p], mwr[j, p])
            left = mb[j, p] - (v - me1[j, p + 1, real, :] + 2.0 * half * total)
            update = v + left * mrd[j, p]
            me2[j + 1, p + 1, real, :] = update
            return pack(slots_mid_two[j], p, update, packed)

        col_send[slots_mid_two[j]] = plane_loop(body, blank)
        halo_send(slots_mid_two[j])
    time_send(4)

    time_wait(4)
    for j in range(2):
        halo_wait(slots_mid_two[j])
    pair = [ghosts(slots_mid_two[j]) for j in range(2)]

    def top_weights(p):
        return 0.5 * (mwl[0, p] + mwl[1, p]), 0.5 * (mwr[0, p] + mwr[1, p])

    def body(p, packed):
        rhs = None
        for j in range(2):
            v, v_near = near_of(me2, j + 1, slots_mid_two[j], pair[j], p)
            total = flux(v, v_near, mc[j, p + 1, real, :], straight(mc, j, p), mwl[j, p], mwr[j, p])
            left = mb[j, p] - (v - me2[j, p + 1, real, :] + 2.0 * half * total)
            rhs = left if rhs is None else rhs + left
        tb[p] = rhs
        update = rhs * diagonal(tc, 0, p, *top_weights(p), 4.0 * half)
        te[1, p + 1, real, :] = update
        return pack(slot_top, p, update, packed)

    col_send[slot_top] = plane_loop(body, blank)
    halo_send(slot_top)
    time_send(5)
    time_wait(5)
    halo_wait(slot_top)
    ghost = ghosts(slot_top)

    def body(p, carry):
        v, v_near = near_of(te, 1, slot_top, ghost, p)
        weights = top_weights(p)
        total = flux(v, v_near, tc[0, p + 1, real, :], straight(tc, 0, p), *weights)
        left = tb[p] - (v - te[0, p + 1, real, :] + 4.0 * half * total)
        update = v + left * diagonal(tc, 0, p, *weights, 4.0 * half)
        for n in range(group):
            mid = me2[n // 2 + 1, p + 1, real, :] + update
            new[n, p] = u[n + 1, p + 1, real, :] + (e2[n + 1, p + 1, real, :] + mid)
        return carry

    plane_loop(body, 0)
    for j in order:
        out_copy(1, j).start()

    for a in range(2):
        for j in order[:3]:
            in_copy(a, j).wait_send()
    for slot, count in [(slot, 2) for slot in slots_state] + [
        (slot, 1) for slot in range(slots_one[0], n_slots)
    ]:
        for number in range(4):

            @pl.when(sides[number][0])
            def _():
                halo_copy(slot, count, number).wait_send()

    if chained:

        @pl.when(has_next)
        def _():
            for number, (ref, last) in enumerate(time_refs):
                time_copy(number, ref, last).wait_send()

    for a in range(2):
        out_copy(a, 0).wait()
        for j in order[:3]:
            out_copy(a, j).wait_send()
            out_copy(a, j).wait_recv()


def shards(tm_size, space_size, iterate, source_term, conductivity):
    _, nz, tx, ty = conductivity.shape
    width = ty // group
    rows = tx + 2 * pad
    f32 = jnp.float32

    def padded(count):
        return pltpu.VMEM((count, nz + 2, rows, width), f32)

    def plain(*lead):
        return pltpu.VMEM((*lead, nz, tx, width), f32)

    dma = pltpu.SemaphoreType.DMA
    out = jax.ShapeDtypeStruct(iterate.shape, f32)
    hbm = pl.BlockSpec(memory_space=pl.ANY)
    return pl.pallas_call(
        functools.partial(kernel, tm_size, space_size),
        out_shape=(out, out),
        in_specs=[hbm] * 3,
        out_specs=(hbm, hbm),
        scratch_shapes=[
            padded(group + 1), padded(group), padded(group + 1), padded(group + 1),
            plain(), plain(group), plain(group), plain(group), plain(group), plain(group),
            padded(2), padded(3), padded(3), plain(2), plain(2), plain(2), plain(2),
            padded(1), padded(2), plain(), plain(group),
            pltpu.VMEM((2, n_slots, nz, width), f32), pltpu.VMEM((2, n_slots, nz, width), f32),
            pltpu.VMEM((n_slots, tx, width), f32), pltpu.VMEM((2, n_slots, tx, width), f32),
            dma((2, group - 1)), dma((2, group - 1)), dma((2, group - 1)), dma((2, group - 1)),
            dma((5,)), dma((4, n_slots)), dma((4, n_slots)), dma((6,)), dma((6,)),
        ],
        compiler_params=pltpu.CompilerParams(
            collective_id=0, has_side_effects=True, vmem_limit_bytes=48 * 2**20
        ),
    )(iterate, source_term, conductivity)


def solution(mesh):
    tiled = P("tm", "space", None, None, None)
    in_specs = (tiled, tiled, P("space", None, None, None))
    body = functools.partial(shards, mesh.shape["tm"], mesh.shape["space"])
    return jax.shard_map(
        body, mesh=mesh, in_specs=in_specs, out_specs=(tiled, tiled), check_vma=False
    )
```

time: 181 us -> 82.7 us (0.46)
  the two profiles are of different devices: /device:TPU:25 before, /device:TPU:0 now
where the time goes in v1:
time: 82.7 us; the launch traced here: 81.8 us
  Pallas kernels  76.5 us (93%)
  local copies, waits for them, and re-layouts  4.71 us (6%)
    pallas_call x1, Pallas kernels, shards(): pl.pallas_call(functools.partial(kernel, tm_size, space_size), out_shape=...  76.5 us
    unnamed x8, local copies, waits for them, and re-layouts  4.71 us

profile of v1, /device:TPU:0, one launch (start us, length us, event | category | flops | bytes accessed | tf_op | source)
XLA Modules:
  0.0 81.8 jit_solution(18381742519506046494)
XLA Ops:
  0.6 0.0 copy-start
  0.6 1.0 %copy-done = f32[1,1,16,16,512]{4,3,2,1,0:T(8,128)S(1)} copy-done((f32[1,1,16,16,512]{4,3,2,1,0:T(8,128)S(1)}, f32[1,1,16,16,512]{4,3,2,1,0:T(8,128)}, u32[]{:S(2)}) %copy-start) | copy-done | bytes 524312
  1.7 0.0 copy-start.1
  1.7 1.0 %copy-done.1 = f32[1,1,16,16,512]{4,3,2,1,0:T(8,128)S(1)} copy-done((f32[1,1,16,16,512]{4,3,2,1,0:T(8,128)S(1)}, f32[1,1,16,16,512]{4,3,2,1,0:T(8,128)}, u32[]{:S(2)}) %copy-start.1) | copy-done | bytes 524312
  2.7 0.0 copy-start.2
  2.7 1.0 %copy-done.2 = f32[1,16,16,512]{3,2,1,0:T(8,128)S(1)} copy-done((f32[1,16,16,512]{3,2,1,0:T(8,128)S(1)}, f32[1,16,16,512]{3,2,1,0:T(8,128)}, u32[]{:S(2)}) %copy-start.2) | copy-done | bytes 524312
  3.8 76.5 %shard_map.50 = (f32[1,1,16,16,512]{4,3,2,1,0:T(8,128)S(1)}, f32[1,1,16,16,512]{4,3,2,1,0:T(8,128)S(1)}) custom-call(f32[1,1,16,16,512]{4,3,2,1,0:T(8,128)S(1)} %copy-done, f32[1,1,16,16,512]{4,3,2,1,0:T(8,128)S(1)} %copy-done.1, f32[1,16,16,512]{3,2,1,0:T(8,128)S(1)} %copy-done.2), custom_call_target="tpu_custom_call" | custom-call | tf_op jit(solution)/shard_map/pallas_call | solution.py:459
  80.2 0.8 copy.7
  81.0 0.8 copy.8
Async XLA Ops:
  0.6 1.0 %copy-start = (f32[1,1,16,16,512]{4,3,2,1,0:T(8,128)S(1)}, f32[1,1,16,16,512]{4,3,2,1,0:T(8,128)}, u32[]{:S(2)}) copy-start(f32[1,1,16,16,512]{4,3,2,1,0:T(8,128)} %state_in.1) | copy-start | bytes 1572868
  1.7 1.0 %copy-start.1 = (f32[1,1,16,16,512]{4,3,2,1,0:T(8,128)S(1)}, f32[1,1,16,16,512]{4,3,2,1,0:T(8,128)}, u32[]{:S(2)}) copy-start(f32[1,1,16,16,512]{4,3,2,1,0:T(8,128)} %source_in.1) | copy-start | bytes 1572868
  2.7 1.0 %copy-start.2 = (f32[1,16,16,512]{3,2,1,0:T(8,128)S(1)}, f32[1,16,16,512]{3,2,1,0:T(8,128)}, u32[]{:S(2)}) copy-start(f32[1,16,16,512]{3,2,1,0:T(8,128)} %kappa_in.1) | copy-start | bytes 1572868

commit v2 on v1

--- a/solution.py
+++ b/solution.py
@@ -20,6 +20,8 @@
 slots_mid_two = [18, 19]
 slot_top = 20
 n_slots = 21
+parts = 4
+pace = {"one": 3, "two": 3, "mid_one": 2, "mid_two": 2, "top": 2}
 
 
 def kernel(
@@ -27,8 +29,8 @@
     state_in, source_in, kappa_in, new_out, res_out,
     u, c, e1, e2, kap, src, res, wl, wr, rd,
     mc, me1, me2, mb, mwl, mwr, mrd, tc, te, tb, new,
-    row_send, row_recv, col_send, col_recv,
-    in_ssem, in_rsem, out_ssem, out_rsem, loc_sem, h_ssem, h_rsem, t_ssem, t_rsem,
+    row_send, row_recv, col_send, col_recv, own, beside, edge_send, edge_recv,
+    in_ssem, in_rsem, out_ssem, out_rsem, out_lsem, e_ssem, e_rsem, loc_sem, h_ssem, h_rsem, t_ssem, t_rsem,
 ):
     nz, tx, width = kap.shape
     real = pl.ds(pad, tx)
@@ -55,6 +57,71 @@
             for plane in (0, nz + 1):
                 ref[n, plane] = jnp.zeros(ref.shape[2:], jnp.float32)
 
+    def columns(d):
+        return pl.ds(pl.multiple_of(d * width, width), width)
+
+    kappa_copy = pltpu.make_async_copy(kappa_in.at[0, :, :, columns(q)], kap, loc_sem.at[2])
+    own_copy = pltpu.make_async_copy(state_in.at[0, 0], own, loc_sem.at[5])
+
+    def beside_copy(side):
+        block = kappa_in.at[0, :, :, columns(q - 1 + 2 * side)]
+        return pltpu.make_async_copy(block, beside.at[side], loc_sem.at[6 + side])
+
+    own_copy.start()
+    kappa_copy.start()
+    for side in range(2):
+
+        @pl.when(sides[2 + side][0])
+        def _():
+            beside_copy(side).start()
+
+    barrier = pltpu.get_barrier_semaphore()
+    for j in range(1, group):
+        pl.semaphore_signal(
+            barrier, inc=1, device_id={"tm": base + (q + j) % group}, device_id_type=mesh_ids
+        )
+    greeted = [(has_dn, sides[0][1]), (has_up, sides[1][1])]
+    if chained:
+        greeted += [(has_prev, {"tm": me - group}), (has_next, {"tm": me + group})]
+    for has, where in greeted:
+
+        @pl.when(has)
+        def _():
+            pl.semaphore_signal(barrier, inc=1, device_id=where, device_id_type=mesh_ids)
+
+    expected = group - 1
+    for has, _ in greeted:
+        expected = expected + jnp.where(has, 1, 0)
+    pl.semaphore_wait(barrier, expected)
+
+    def in_copy(a, j):
+        d = (q + j) % group
+        hbm = (state_in, source_in)[a].at[0, 0, :, :, columns(d)]
+        dst = u.at[q + 1, planes, real, :] if a == 0 else src.at[q]
+        if j == 0:
+            return pltpu.make_async_copy(hbm, dst, loc_sem.at[a])
+        return pltpu.make_async_remote_copy(
+            src_ref=hbm, dst_ref=dst, send_sem=in_ssem.at[a, j - 1],
+            recv_sem=in_rsem.at[a, j - 1], device_id={"tm": base + d}, device_id_type=mesh_ids,
+        )
+
+    def out_copy(a, j, part):
+        d = (q + j) % group
+        some = pl.ds(part * (nz // parts), nz // parts)
+        hbm = (res_out, new_out)[a].at[0, 0, some, :, columns(q)]
+        held = (res, new)[a].at[d, some]
+        if j == 0:
+            return pltpu.make_async_copy(held, hbm, out_lsem.at[a, part])
+        return pltpu.make_async_remote_copy(
+            src_ref=held, dst_ref=hbm, send_sem=out_ssem.at[a, part, j - 1],
+            recv_sem=out_rsem.at[a, part, j - 1], device_id={"tm": base + d},
+            device_id_type=mesh_ids,
+        )
+
+    order = (2, 1, 3, 0)
+    for j in order:
+        in_copy(0, j).start()
+
     zero_edges(u, group + 1)
     zero_edges(c, group)
     zero_edges(e1, group + 1)
@@ -77,58 +144,49 @@
         def _():
             buffer[number % 2] = jnp.zeros(buffer.shape[1:], jnp.float32)
 
-    barrier = pltpu.get_barrier_semaphore()
-    for j in range(1, group):
-        pl.semaphore_signal(
-            barrier, inc=1, device_id={"tm": base + (q + j) % group}, device_id_type=mesh_ids
-        )
-    greeted = [(has_dn, sides[0][1]), (has_up, sides[1][1])]
-    if chained:
-        greeted += [(has_prev, {"tm": me - group}), (has_next, {"tm": me + group})]
-    for has, where in greeted:
-
-        @pl.when(has)
+    for side in range(2):
+
+        @pl.when(jnp.logical_not(sides[2 + side][0]))
         def _():
-            pl.semaphore_signal(barrier, inc=1, device_id=where, device_id_type=mesh_ids)
-
-    expected = group - 1
-    for has, _ in greeted:
-        expected = expected + jnp.where(has, 1, 0)
-    pl.semaphore_wait(barrier, expected)
-
-    def columns(d):
-        return pl.ds(pl.multiple_of(d * width, width), width)
-
-    def in_copy(a, j):
+            beside[side] = jnp.zeros(beside.shape[1:], jnp.float32)
+
+    lane = lax.broadcasted_iota(jnp.int32, (tx, width), 1)
+    blank = jnp.zeros((tx, width), jnp.float32)
+
+    def pack_sides(p, left, right, packed):
+        if left is not None:
+            packed = jnp.where(lane == 2 * p + 1, pltpu.roll(left, 2 * p + 2, 1), packed)
+        if right is not None:
+            packed = jnp.where(lane == 2 * p, pltpu.roll(right, 2 * p, 1), packed)
+        return packed
+
+    def pack_body(p, packed):
+        blocks = [own[p, :, d * width : (d + 1) * width] for d in range(group)]
+        return tuple(
+            pack_sides(
+                p, blocks[d - 1] if d else None,
+                blocks[d + 1] if d < group - 1 else None, packed[d],
+            )
+            for d in range(group)
+        )
+
+    own_copy.wait()
+    packed = lax.fori_loop(0, nz, pack_body, (blank,) * group, unroll=4)
+    for d in range(group):
+        edge_send[d] = packed[d]
+    edge_recv[q] = edge_send[q]
+
+    def edge_copy(j):
         d = (q + j) % group
-        hbm = (state_in, source_in)[a].at[0, 0, :, :, columns(d)]
-        dst = u.at[q + 1, planes, real, :] if a == 0 else src.at[q]
-        if j == 0:
-            return pltpu.make_async_copy(hbm, dst, loc_sem.at[a])
         return pltpu.make_async_remote_copy(
-            src_ref=hbm, dst_ref=dst, send_sem=in_ssem.at[a, j - 1],
-            recv_sem=in_rsem.at[a, j - 1], device_id={"tm": base + d}, device_id_type=mesh_ids,
-        )
-
-    def out_copy(a, j):
-        d = (q + j) % group
-        hbm = (res_out, new_out)[a].at[0, 0, :, :, columns(q)]
-        own = (res, new)[a].at[d]
-        if j == 0:
-            return pltpu.make_async_copy(own, hbm, loc_sem.at[3 + a])
-        return pltpu.make_async_remote_copy(
-            src_ref=own, dst_ref=hbm, send_sem=out_ssem.at[a, j - 1],
-            recv_sem=out_rsem.at[a, j - 1], device_id={"tm": base + d}, device_id_type=mesh_ids,
-        )
-
-    kappa_copy = pltpu.make_async_copy(
-        kappa_in.at[0, :, :, columns(q)], kap, loc_sem.at[2]
-    )
-    kappa_copy.start()
-    order = (2, 1, 3, 0)
-    for a in range(2):
-        for j in order:
-            in_copy(a, j).start()
+            src_ref=edge_send.at[d], dst_ref=edge_recv.at[q], send_sem=e_ssem.at[j - 1],
+            recv_sem=e_rsem.at[j - 1], device_id={"tm": base + d}, device_id_type=mesh_ids,
+        )
+
+    for j in order[:3]:
+        edge_copy(j).start()
+    for j in order:
+        in_copy(1, j).start()
 
     def halo_copy(slot, count, number):
         part = pl.ds(slot, count)
@@ -143,16 +201,16 @@
             device_id_type=mesh_ids,
         )
 
-    def halo_send(slot, count=1):
-        for number in (2, 3, 0, 1):
+    def halo_send(slot, count=1, which=(2, 3, 0, 1)):
+        for number in which:
 
             @pl.when(sides[number][0])
             def _():
                 halo_copy(slot, count, number).start()
 
-    def halo_wait(slot, count=1):
+    def halo_wait(slot, count=1, which=(2, 3, 0, 1)):
         part = pl.ds(slot, count)
-        for number in range(4):
+        for number in which:
             target = row_recv.at[number, part] if number < 2 else col_recv.at[number - 2, part]
 
             @pl.when(sides[number][0])
@@ -186,15 +244,17 @@
             def _():
                 time_copy(number, *time_refs[number]).wait_recv()
 
-    lane = lax.broadcasted_iota(jnp.int32, (tx, width), 1)
     first_lane = lane == 0
     last_lane = lane == width - 1
     odd_lane = lane % 2 == 1
     pair_lane = lane // 2
 
-    def pack(slot, p, value, packed):
+    def put_send(slot, p, value):
         row_send[0, slot, pl.ds(p, 1), :] = value[:1]
         row_send[1, slot, pl.ds(p, 1), :] = value[tx - 1 :]
+
+    def pack(slot, p, value, packed):
+        put_send(slot, p, value)
         return jnp.where(pair_lane == p, pltpu.roll(value, 2 * p + 1, 1), packed)
 
     def ghosts(slot):
@@ -232,9 +292,18 @@
         return v, straight(ref, n, p) + sideways(v, ghost, p)
 
     def plane_loop(body, init):
-        return lax.fori_loop(0, nz, body, init, unroll=2)
-
-    blank = jnp.zeros((tx, width), jnp.float32)
+        return lax.fori_loop(0, nz, body, init, unroll=8)
+
+    for side in range(2):
+
+        @pl.when(sides[2 + side][0])
+        def _():
+            beside_copy(side).wait()
+
+    def kappa_body(p, packed):
+        return pack_sides(p, beside[0, p], beside[1, p], packed)
+
+    kappa_edge = lax.fori_loop(0, nz, kappa_body, blank, unroll=4)
 
     kappa_copy.wait()
     in_copy(0, 0).wait()
@@ -243,22 +312,23 @@
     time_send(0)
     for n in range(group):
 
-        def body(p, packed):
+        def body(p, carry):
             v = u[n + 1, p + 1, real, :]
             cc = kap[p] * (1.0 + v * v)
             c[n, p + 1, real, :] = cc
-            slot = slots_state[n]
-            return pack(slot, p, v, packed[0]), pack(slot + 1, p, cc, packed[1])
-
-        packed = plane_loop(body, (blank, blank))
-        col_send[slots_state[n]] = packed[0]
-        col_send[slots_state[n] + 1] = packed[1]
-        halo_send(slots_state[n], 2)
-
+            put_send(slots_state[n], p, v)
+            put_send(slots_state[n] + 1, p, cc)
+            return carry
+
+        plane_loop(body, 0)
+        halo_send(slots_state[n], 2, (0, 1))
+
+    for j in order[:3]:
+        edge_copy(j).wait_recv()
     half = 0.5 * tau_step
     for n in range(group):
-        halo_wait(slots_state[n], 2)
-        ghost_c = ghosts(slots_state[n] + 1)
+        halo_wait(slots_state[n], 2, (0, 1))
+        ghost_c = kappa_edge * (1.0 + edge_recv[n] * edge_recv[n])
 
         def body(p, carry):
             cc, c_near = near_of(c, n, slots_state[n] + 1, ghost_c, p)
@@ -277,7 +347,7 @@
         in_copy(1, j).wait_recv()
     time_wait(0)
     for n in range(group):
-        ghost_u = ghosts(slots_state[n])
+        ghost_u = edge_recv[n]
 
         def body(p, packed):
             v, v_near = near_of(u, n + 1, slots_state[n], ghost_u, p)
@@ -292,8 +362,16 @@
         halo_send(slots_one[n])
     time_send(1)
 
-    for j in order:
-        out_copy(0, j).start()
+    pieces = [(j, part) for part in range(parts) for j in order]
+    remote_pieces = [piece for piece in pieces if piece[0]]
+    for part in range(parts):
+        out_copy(0, 0, part).start()
+
+    def give(stage):
+        for _ in range(pace[stage]):
+            out_copy(0, *remote_pieces.pop(0)).start()
+
+    give("one")
 
     time_wait(1)
     for n in range(group):
@@ -311,6 +389,7 @@
         col_send[slots_two[n]] = plane_loop(body, blank)
         halo_send(slots_two[n])
     time_send(2)
+    give("two")
 
     def body(p, carry):
         for j in range(2):
@@ -355,6 +434,7 @@
         col_send[slots_mid_one[j]] = plane_loop(body, blank)
         halo_send(slots_mid_one[j])
     time_send(3)
+    give("mid_one")
 
     time_wait(3)
     for j in range(2):
@@ -372,6 +452,7 @@
         col_send[slots_mid_two[j]] = plane_loop(body, blank)
         halo_send(slots_mid_two[j])
     time_send(4)
+    give("mid_two")
 
     time_wait(4)
     for j in range(2):
@@ -396,6 +477,7 @@
     col_send[slot_top] = plane_loop(body, blank)
     halo_send(slot_top)
     time_send(5)
+    give("top")
     time_wait(5)
     halo_wait(slot_top)
     ghost = ghosts(slot_top)
@@ -411,17 +493,22 @@
             new[n, p] = u[n + 1, p + 1, real, :] + (e2[n + 1, p + 1, real, :] + mid)
         return carry
 
-    plane_loop(body, 0)
-    for j in order:
-        out_copy(1, j).start()
+    for part in range(parts):
+        first = part * (nz // parts)
+        lax.fori_loop(first, first + nz // parts, body, 0, unroll=True)
+        for j in order:
+            out_copy(1, j, part).start()
+
+    for j in order[:3]:
+        edge_copy(j).wait_send()
 
     for a in range(2):
         for j in order[:3]:
             in_copy(a, j).wait_send()
-    for slot, count in [(slot, 2) for slot in slots_state] + [
-        (slot, 1) for slot in range(slots_one[0], n_slots)
-    ]:
-        for number in range(4):
+    halos = [(slot, 2, (0, 1)) for slot in slots_state]
+    halos += [(slot, 1, (0, 1, 2, 3)) for slot in range(slots_one[0], n_slots)]
+    for slot, count, which in halos:
+        for number in which:
 
             @pl.when(sides[number][0])
             def _():
@@ -435,10 +522,12 @@
                 time_copy(number, ref, last).wait_send()
 
     for a in range(2):
-        out_copy(a, 0).wait()
-        for j in order[:3]:
-            out_copy(a, j).wait_send()
-            out_copy(a, j).wait_recv()
+        for j, part in pieces:
+            if j == 0:
+                out_copy(a, j, part).wait()
+            else:
+                out_copy(a, j, part).wait_send()
+                out_copy(a, j, part).wait_recv()
 
 
 def shards(tm_size, space_size, iterate, source_term, conductivity):
@@ -455,7 +544,7 @@
 
     dma = pltpu.SemaphoreType.DMA
     out = jax.ShapeDtypeStruct(iterate.shape, f32)
-    hbm = pl.BlockSpec(memory_space=pl.ANY)
+    hbm = pl.BlockSpec(memory_space=pltpu.HBM)
     return pl.pallas_call(
         functools.partial(kernel, tm_size, space_size),
         out_shape=(out, out),
@@ -468,8 +557,11 @@
             padded(1), padded(2), plain(), plain(group),
             pltpu.VMEM((2, n_slots, nz, width), f32), pltpu.VMEM((2, n_slots, nz, width), f32),
             pltpu.VMEM((n_slots, tx, width), f32), pltpu.VMEM((2, n_slots, tx, width), f32),
-            dma((2, group - 1)), dma((2, group - 1)), dma((2, group - 1)), dma((2, group - 1)),
-            dma((5,)), dma((4, n_slots)), dma((4, n_slots)), dma((6,)), dma((6,)),
+            pltpu.VMEM((nz, tx, ty), f32), plain(2),
+            pltpu.VMEM((group, tx, width), f32), pltpu.VMEM((group, tx, width), f32),
+            dma((2, group - 1)), dma((2, group - 1)),
+            dma((2, parts, group - 1)), dma((2, parts, group - 1)), dma((2, parts)),
+            dma((group - 1,)), dma((group - 1,)), dma((8,)), dma((4, n_slots)), dma((4, n_slots)), dma((6,)), dma((6,)),
         ],
         compiler_params=pltpu.CompilerParams(
             collective_id=0, has_side_effects=True, vmem_limit_bytes=48 * 2**20

time: 82.7 us -> 68.8 us (0.83)
  Pallas kernels: 76.5 us -> 63.2 us
    pallas_call x1, Pallas kernels: 76.5 us -> 63.2 us  [shards(): pl.pallas_call(functools.partial(kernel, tm_size, space_size), out_shape=...]
where the time goes in v2:
time: 68.8 us; the launch traced here: 68.6 us
  Pallas kernels  63.2 us (92%)
  local copies, waits for them, and re-layouts  4.71 us (7%)
    pallas_call x1, Pallas kernels, shards(): pl.pallas_call(functools.partial(kernel, tm_size, space_size), out_shape=...  63.2 us
    unnamed x8, local copies, waits for them, and re-layouts  4.71 us

profile of v2, /device:TPU:0, one launch (start us, length us, event | category | flops | bytes accessed | tf_op | source)
XLA Modules:
  0.0 68.6 jit_solution(9181686417629917942)
XLA Ops:
  0.6 0.0 copy-start
  0.6 1.0 %copy-done = f32[1,1,16,16,512]{4,3,2,1,0:T(8,128)S(1)} copy-done((f32[1,1,16,16,512]{4,3,2,1,0:T(8,128)S(1)}, f32[1,1,16,16,512]{4,3,2,1,0:T(8,128)}, u32[]{:S(2)}) %copy-start) | copy-done | bytes 524312
  1.7 0.0 copy-start.1
  1.7 1.0 %copy-done.1 = f32[1,1,16,16,512]{4,3,2,1,0:T(8,128)S(1)} copy-done((f32[1,1,16,16,512]{4,3,2,1,0:T(8,128)S(1)}, f32[1,1,16,16,512]{4,3,2,1,0:T(8,128)}, u32[]{:S(2)}) %copy-start.1) | copy-done | bytes 524312
  2.7 0.0 copy-start.2
  2.7 1.0 %copy-done.2 = f32[1,16,16,512]{3,2,1,0:T(8,128)S(1)} copy-done((f32[1,16,16,512]{3,2,1,0:T(8,128)S(1)}, f32[1,16,16,512]{3,2,1,0:T(8,128)}, u32[]{:S(2)}) %copy-start.2) | copy-done | bytes 524312
  3.8 63.2 %shard_map.50 = (f32[1,1,16,16,512]{4,3,2,1,0:T(8,128)S(1)}, f32[1,1,16,16,512]{4,3,2,1,0:T(8,128)S(1)}) custom-call(f32[1,1,16,16,512]{4,3,2,1,0:T(8,128)S(1)} %copy-done, f32[1,1,16,16,512]{4,3,2,1,0:T(8,128)S(1)} %copy-done.1, f32[1,16,16,512]{3,2,1,0:T(8,128)S(1)} %copy-done.2), custom_call_target="tpu_custom_call" | custom-call | tf_op jit(solution)/shard_map/pallas_call | solution.py:548
  67.0 0.8 %copy.7 = f32[1,1,16,16,512]{4,3,2,1,0:T(8,128)} copy(f32[1,1,16,16,512]{4,3,2,1,0:T(8,128)S(1)} %get-tuple-element.4) | data formatting | bytes 1048576
  67.8 0.8 %copy.8 = f32[1,1,16,16,512]{4,3,2,1,0:T(8,128)} copy(f32[1,1,16,16,512]{4,3,2,1,0:T(8,128)S(1)} %get-tuple-element.5) | data formatting | bytes 1048576
Async XLA Ops:
  0.6 1.0 %copy-start = (f32[1,1,16,16,512]{4,3,2,1,0:T(8,128)S(1)}, f32[1,1,16,16,512]{4,3,2,1,0:T(8,128)}, u32[]{:S(2)}) copy-start(f32[1,1,16,16,512]{4,3,2,1,0:T(8,128)} %state_in.1) | copy-start | bytes 1572868
  1.7 1.0 %copy-start.1 = (f32[1,1,16,16,512]{4,3,2,1,0:T(8,128)S(1)}, f32[1,1,16,16,512]{4,3,2,1,0:T(8,128)}, u32[]{:S(2)}) copy-start(f32[1,1,16,16,512]{4,3,2,1,0:T(8,128)} %source_in.1) | copy-start | bytes 1572868
  2.7 1.0 %copy-start.2 = (f32[1,16,16,512]{3,2,1,0:T(8,128)S(1)}, f32[1,16,16,512]{3,2,1,0:T(8,128)}, u32[]{:S(2)}) copy-start(f32[1,16,16,512]{3,2,1,0:T(8,128)} %kappa_in.1) | copy-start | bytes 1572868

commit v3 on v2

--- a/solution.py
+++ b/solution.py
@@ -20,8 +20,8 @@
 slots_mid_two = [18, 19]
 slot_top = 20
 n_slots = 21
-parts = 4
-pace = {"one": 3, "two": 3, "mid_one": 2, "mid_two": 2, "top": 2}
+parts = 2
+pace = {"one": 1, "two": 2, "mid_one": 1, "mid_two": 1, "top": 1}
 
 
 def kernel(
@@ -30,7 +30,7 @@
     u, c, e1, e2, kap, src, res, wl, wr, rd,
     mc, me1, me2, mb, mwl, mwr, mrd, tc, te, tb, new,
     row_send, row_recv, col_send, col_recv, own, beside, edge_send, edge_recv,
-    in_ssem, in_rsem, out_ssem, out_rsem, out_lsem, e_ssem, e_rsem, loc_sem, h_ssem, h_rsem, t_ssem, t_rsem,
+    in_ssem, in_rsem, out_ssem, out_rsem, out_lsem, in_lsem, e_ssem, e_rsem, loc_sem, h_ssem, h_rsem, t_ssem, t_rsem,
 ):
     nz, tx, width = kap.shape
     real = pl.ds(pad, tx)
@@ -96,10 +96,13 @@
 
     def in_copy(a, j):
         d = (q + j) % group
-        hbm = (state_in, source_in)[a].at[0, 0, :, :, columns(d)]
-        dst = u.at[q + 1, planes, real, :] if a == 0 else src.at[q]
+        if a == 0:
+            hbm, dst = state_in.at[0, 0, :, :, columns(d)], u.at[q + 1, planes, real, :]
+        else:
+            some = pl.ds((a - 1) * (nz // parts), nz // parts)
+            hbm, dst = source_in.at[0, 0, some, :, columns(d)], src.at[q, some]
         if j == 0:
-            return pltpu.make_async_copy(hbm, dst, loc_sem.at[a])
+            return pltpu.make_async_copy(hbm, dst, in_lsem.at[a])
         return pltpu.make_async_remote_copy(
             src_ref=hbm, dst_ref=dst, send_sem=in_ssem.at[a, j - 1],
             recv_sem=in_rsem.at[a, j - 1], device_id={"tm": base + d}, device_id_type=mesh_ids,
@@ -185,8 +188,9 @@
 
     for j in order[:3]:
         edge_copy(j).start()
-    for j in order:
-        in_copy(1, j).start()
+    for part in range(parts):
+        for j in order:
+            in_copy(1 + part, j).start()
 
     def halo_copy(slot, count, number):
         part = pl.ds(slot, count)
@@ -323,6 +327,7 @@
         plane_loop(body, 0)
         halo_send(slots_state[n], 2, (0, 1))
 
+    time_wait(0)
     for j in order[:3]:
         edge_copy(j).wait_recv()
     half = 0.5 * tau_step
@@ -330,36 +335,43 @@
         halo_wait(slots_state[n], 2, (0, 1))
         ghost_c = kappa_edge * (1.0 + edge_recv[n] * edge_recv[n])
 
+        ghost_u = edge_recv[n]
+
         def body(p, carry):
             cc, c_near = near_of(c, n, slots_state[n] + 1, ghost_c, p)
-            wl[n, p] = cc + c_near[4]
-            wr[n, p] = cc + c_near[5]
+            left_w, right_w = cc + c_near[4], cc + c_near[5]
+            wl[n, p], wr[n, p] = left_w, right_w
             total = 6.0 * cc
             for item in c_near:
                 total = total + item
             rd[n, p] = damping / (1.0 + half * total)
+            v, v_near = near_of(u, n + 1, slots_state[n], ghost_u, p)
+            total = flux(v, v_near, cc, c_near, left_w, right_w)
+            res[n, p] = v - u[n, p + 1, real, :] + half * total
             return carry
 
         plane_loop(body, 0)
 
-    in_copy(1, 0).wait()
-    for j in order[:3]:
-        in_copy(1, j).wait_recv()
-    time_wait(0)
-    for n in range(group):
-        ghost_u = edge_recv[n]
-
-        def body(p, packed):
-            v, v_near = near_of(u, n + 1, slots_state[n], ghost_u, p)
-            total = flux(v, v_near, c[n, p + 1, real, :], straight(c, n, p), wl[n, p], wr[n, p])
-            left = src[n, p] - (v - u[n, p + 1, real, :] + half * total)
-            res[n, p] = left
-            update = left * rd[n, p]
-            e1[n + 1, p + 1, real, :] = update
-            return pack(slots_one[n], p, update, packed)
-
-        col_send[slots_one[n]] = plane_loop(body, blank)
-        halo_send(slots_one[n])
+    for part in range(parts):
+        in_copy(1 + part, 0).wait()
+        for j in order[:3]:
+            in_copy(1 + part, j).wait_recv()
+        for n in range(group):
+
+            def body(p, packed):
+                left = src[n, p] - res[n, p]
+                res[n, p] = left
+                update = left * rd[n, p]
+                e1[n + 1, p + 1, real, :] = update
+                return pack(slots_one[n], p, update, packed)
+
+            first = part * (nz // parts)
+            packed = col_send[slots_one[n]] if part else blank
+            col_send[slots_one[n]] = lax.fori_loop(
+                first, first + nz // parts, body, packed, unroll=True
+            )
+            if part == parts - 1:
+                halo_send(slots_one[n])
     time_send(1)
 
     pieces = [(j, part) for part in range(parts) for j in order]
@@ -502,7 +514,7 @@
     for j in order[:3]:
         edge_copy(j).wait_send()
 
-    for a in range(2):
+    for a in range(1 + parts):
         for j in order[:3]:
             in_copy(a, j).wait_send()
     halos = [(slot, 2, (0, 1)) for slot in slots_state]
@@ -559,12 +571,12 @@
             pltpu.VMEM((n_slots, tx, width), f32), pltpu.VMEM((2, n_slots, tx, width), f32),
             pltpu.VMEM((nz, tx, ty), f32), plain(2),
             pltpu.VMEM((group, tx, width), f32), pltpu.VMEM((group, tx, width), f32),
-            dma((2, group - 1)), dma((2, group - 1)),
-            dma((2, parts, group - 1)), dma((2, parts, group - 1)), dma((2, parts)),
+            dma((1 + parts, group - 1)), dma((1 + parts, group - 1)),
+            dma((2, parts, group - 1)), dma((2, parts, group - 1)), dma((2, parts)), dma((1 + parts,)),
             dma((group - 1,)), dma((group - 1,)), dma((8,)), dma((4, n_slots)), dma((4, n_slots)), dma((6,)), dma((6,)),
         ],
         compiler_params=pltpu.CompilerParams(
-            collective_id=0, has_side_effects=True, vmem_limit_bytes=48 * 2**20
+            collective_id=0, has_side_effects=True, vmem_limit_bytes=67043328
         ),
     )(iterate, source_term, conductivity)
 

time: 68.8 us -> 66.3 us (0.964)
  local copies, waits for them, and re-layouts: 4.71 us -> 2.74 us
    unnamed x8 -> x4, local copies, waits for them, and re-layouts: 4.71 us -> 2.74 us
where the time goes in v3:
time: 66.3 us; the launch traced here: 66.1 us
  Pallas kernels  62.8 us (95%)
  local copies, waits for them, and re-layouts  2.74 us (4%)
    pallas_call x1, Pallas kernels, shards(): pl.pallas_call(functools.partial(kernel, tm_size, space_size), out_shape=...  62.8 us
    unnamed x4, local copies, waits for them, and re-layouts  2.74 us

profile of v3, /device:TPU:0, one launch (start us, length us, event | category | flops | bytes accessed | tf_op | source)
XLA Modules:
  0.0 66.1 jit_solution(12271609260361164955)
XLA Ops:
  0.6 62.8 %shard_map.50 = (f32[1,1,16,16,512]{4,3,2,1,0:T(8,128)}, f32[1,1,16,16,512]{4,3,2,1,0:T(8,128)}) custom-call(f32[1,1,16,16,512]{4,3,2,1,0:T(8,128)} %state_in.1, f32[1,1,16,16,512]{4,3,2,1,0:T(8,128)} %source_in.1, f32[1,16,16,512]{3,2,1,0:T(8,128)} %kappa_in.1), custom_call_target="tpu_custom_call" | custom-call | tf_op jit(solution)/shard_map/pallas_call | solution.py:560
  63.4 0.0 copy-start
  63.4 1.9 %copy.7 = f32[1,1,16,16,512]{4,3,2,1,0:T(8,128)} copy(f32[1,1,16,16,512]{4,3,2,1,0:T(8,128)} %get-tuple-element.4) | data formatting | bytes 1048576
  65.4 0.0 copy-done
  65.4 0.8 %copy.8 = f32[1,1,16,16,512]{4,3,2,1,0:T(8,128)} copy(f32[1,1,16,16,512]{4,3,2,1,0:T(8,128)S(1)} %copy-done) | data formatting | bytes 1048576
Async XLA Ops:
  63.4 2.0 %copy-start = (f32[1,1,16,16,512]{4,3,2,1,0:T(8,128)S(1)}, f32[1,1,16,16,512]{4,3,2,1,0:T(8,128)}, u32[]{:S(2)}) copy-start(f32[1,1,16,16,512]{4,3,2,1,0:T(8,128)} %get-tuple-element.5) | copy-start | bytes 1572868

commit v4 on v3

--- a/solution.py
+++ b/solution.py
@@ -21,7 +21,7 @@
 slot_top = 20
 n_slots = 21
 parts = 2
-pace = {"one": 1, "two": 2, "mid_one": 1, "mid_two": 1, "top": 1}
+pace = {"one": 2, "two": 1, "mid_one": 1, "mid_two": 1, "top": 1}
 
 
 def kernel(

time: 66.3 us -> 65.7 us (level); the launches traced: 66.1 us -> 64.5 us
  Pallas kernels: 62.8 us -> 61.2 us
    pallas_call x1, Pallas kernels: 62.8 us -> 61.2 us  [shards(): pl.pallas_call(functools.partial(kernel, tm_size, space_size), out_shape=...]
where the time goes in v4:
time: 65.7 us; the launch traced here: 64.5 us
  Pallas kernels  61.2 us (93%)
  local copies, waits for them, and re-layouts  2.74 us (4%)
    pallas_call x1, Pallas kernels, shards(): pl.pallas_call(functools.partial(kernel, tm_size, space_size), out_shape=...  61.2 us
    unnamed x4, local copies, waits for them, and re-layouts  2.74 us

profile of v4, /device:TPU:0, one launch (start us, length us, event | category | flops | bytes accessed | tf_op | source)
XLA Modules:
  0.0 64.5 jit_solution(17059818354720840332)
XLA Ops:
  0.6 61.2 %shard_map.50 = (f32[1,1,16,16,512]{4,3,2,1,0:T(8,128)}, f32[1,1,16,16,512]{4,3,2,1,0:T(8,128)}) custom-call(f32[1,1,16,16,512]{4,3,2,1,0:T(8,128)} %state_in.1, f32[1,1,16,16,512]{4,3,2,1,0:T(8,128)} %source_in.1, f32[1,16,16,512]{3,2,1,0:T(8,128)} %kappa_in.1), custom_call_target="tpu_custom_call" | custom-call | tf_op jit(solution)/shard_map/pallas_call | solution.py:560
  61.8 0.0 copy-start
  61.8 1.9 %copy.7 = f32[1,1,16,16,512]{4,3,2,1,0:T(8,128)} copy(f32[1,1,16,16,512]{4,3,2,1,0:T(8,128)} %get-tuple-element.4) | data formatting | bytes 1048576
  63.7 0.0 copy-done
  63.7 0.8 %copy.8 = f32[1,1,16,16,512]{4,3,2,1,0:T(8,128)} copy(f32[1,1,16,16,512]{4,3,2,1,0:T(8,128)S(1)} %copy-done) | data formatting | bytes 1048576
Async XLA Ops:
  61.8 2.0 %copy-start = (f32[1,1,16,16,512]{4,3,2,1,0:T(8,128)S(1)}, f32[1,1,16,16,512]{4,3,2,1,0:T(8,128)}, u32[]{:S(2)}) copy-start(f32[1,1,16,16,512]{4,3,2,1,0:T(8,128)} %get-tuple-element.5) | copy-start | bytes 1572868
